TPU v7x, 256 devices: a whole 4x4x8 slice. The times are simulated.
256 devices in a mesh: chan: 4 (over x), mset: 8 (over y, core), blk: 8 (over z).
Axes of the slice: x: 4, y: 4, z: 8, core: 2. Of those that a mesh axis runs over, the one named last changes fastest.
Arguments:
- harmonics: bfloat16 [2, 3, 64, 1536], P(None, None, ('mset', 'blk'), 'chan'), may hold values from -6 to 6
- mixing: float32 [12, 3], replicated, may hold values from 0.2 to 1.2
- beam_window: float32 [12, 1536], P(None, 'chan'), may hold values from 0.2 to 1
- prior_inv: float32 [3, 1536], P(None, 'chan'), may hold values from 0.3 to 3
- legendre: bfloat16 [64, 1536, 8192], P(('mset', 'blk'), 'chan'), may hold values from -0.15625 to 0.15625
- inv_noise: bfloat16 [12, 8192, 8192], P('chan', ('mset', 'blk')), may hold values from 0.0099487305 to 0.099609375
- mode_index: int32 [64], replicated, may hold values from 0 to 1535, as said below
- cycle_pixels: int32 [12], replicated, may hold values from 2048 to 8192, as said below
Outputs:
- applied: float32 [2, 3, 64, 1536], P(None, None, ('mset', 'blk'), 'chan')
Inputs may be any that keep to these rules, and one draw needn't show every extreme that they name: `mode_index`: distinct values; 0 and 1535 are always among them. `cycle_pixels`: each value is 2048, 4096 or 8192; every draw holds both the smallest and the largest.
All inputs are finite; a program needn't handle non-finite values.
Results may differ from a plain program's by a relative error of at most 0.005.
Values may be sent and summed in bfloat16 or wider, within the bound.
No kernel may reach another device: no remote copies, remote signals or barrier semaphores. Data moves between devices by JAX's collectives and lax.ppermute only.
A program may use at most 128 MiB of HBM per device.

v0:
```python
import math
import jax
import jax.numpy as jnp
from jax import lax
from jax.sharding import PartitionSpec as P


def make_table(mode_index, npix, pixels, mode_count):
    fine_width = 128
    coarse_count = pixels // fine_width
    twice = 2 * npix
    coarse_idx = jnp.arange(coarse_count)
    fine_idx = jnp.arange(fine_width)
    coarse_res = mode_index[:, None] * (2 * fine_width * coarse_idx)[None, :] % twice
    fine_res = mode_index[:, None] * (2 * fine_idx + 1)[None, :] % twice
    scale = jnp.pi / npix.astype(jnp.float32)
    coarse_phase = scale * coarse_res.astype(jnp.float32)
    fine_phase = scale * fine_res.astype(jnp.float32)
    coarse_cos = jnp.cos(coarse_phase)[:, :, None]
    coarse_sin = jnp.sin(coarse_phase)[:, :, None]
    fine_cos = jnp.cos(fine_phase)[:, None, :]
    fine_sin = jnp.sin(fine_phase)[:, None, :]
    cos_full = (coarse_cos * fine_cos - coarse_sin * fine_sin).reshape(mode_count, pixels)
    sin_full = (coarse_sin * fine_cos + coarse_cos * fine_sin).reshape(mode_count, pixels)
    pix_index = jnp.arange(pixels)
    inside = pix_index[None, :] < npix
    weight = jnp.where(mode_index == 0, 1.0, 2.0).astype(jnp.float32)[:, None] / math.sqrt(
        2 * mode_count
    )
    cos_part = jnp.where(inside, weight * cos_full, 0.0)
    sin_part = jnp.where(inside, -weight * sin_full, 0.0)
    return jnp.concatenate([cos_part, sin_part], axis=0).astype(jnp.bfloat16)


def on_device(
    harmonics, mixing, beam_window, prior_inv, legendre, inv_noise, mode_index, cycle_pixels
):
    chan_count = lax.axis_size("chan")
    chan_pos = lax.axis_index("chan")
    chan_slots = inv_noise.shape[0]
    cycle_dev = inv_noise.shape[1]
    pixels = inv_noise.shape[2]
    channels = mixing.shape[0]
    mode_shard = legendre.shape[0]
    local_deg = legendre.shape[1]
    mode_count = mode_index.shape[0]
    total_deg = local_deg * chan_count
    degrees = chan_pos * local_deg + jnp.arange(local_deg)
    band_limit = total_deg * cycle_pixels // pixels - 1
    filter_bank = jnp.where(degrees[None, :] <= band_limit[:, None], beam_window, 0.0)
    coeffs = harmonics.astype(jnp.float32)
    mixture = (
        jnp.sum(mixing[:, None, :, None, None] * coeffs[None], axis=2)
        * filter_bank[:, None, None, :]
    )
    channel_harmonic_coeffs = mixture.astype(jnp.bfloat16).reshape(
        2 * channels, mode_shard, local_deg
    )
    partial_value = jnp.einsum(
        "ijn,jnw->ijw", channel_harmonic_coeffs, legendre, preferred_element_type=jnp.float32
    )
    reduced_sum = lax.psum_scatter(
        partial_value.astype(jnp.bfloat16), "chan", scatter_dimension=0, tiled=True
    )
    cycle_data = lax.all_to_all(
        reduced_sum, ("mset", "blk"), split_axis=2, concat_axis=1, tiled=True
    )
    own_pixels = lax.dynamic_slice_in_dim(cycle_pixels, chan_pos * chan_slots, chan_slots)
    tables = jax.vmap(lambda npix: make_table(mode_index, npix, pixels, mode_count))(own_pixels)
    spectra = cycle_data.reshape(chan_slots, 2 * mode_count, cycle_dev)
    sky_map = jnp.einsum("cnr,cnp->crp", spectra, tables, preferred_element_type=jnp.float32)
    noisy_map = (sky_map * inv_noise).astype(jnp.bfloat16)
    mode_spectra = jnp.einsum("cnp,crp->cnr", tables, noisy_map, preferred_element_type=jnp.float32)
    mode_spectra = mode_spectra.astype(jnp.bfloat16).reshape(2 * chan_slots, mode_count, cycle_dev)
    returned = lax.all_to_all(
        mode_spectra, ("mset", "blk"), split_axis=1, concat_axis=2, tiled=True
    )
    collected_rows = lax.all_gather(returned, "chan", axis=0, tiled=True)
    harmonic_back = jnp.einsum(
        "ogb,gfb->ogf", collected_rows, legendre, preferred_element_type=jnp.float32
    )
    harmonic_back = harmonic_back.reshape(channels, 2, mode_shard, local_deg)
    weighted = harmonic_back * filter_bank[:, None, None, :]
    transposed = jnp.einsum("ck,ciml->ikml", mixing, weighted, precision=lax.Precision.HIGHEST)
    return prior_inv[None, :, None, :] * coeffs + transposed


def solution(mesh):
    placed = (
        P(None, None, ("mset", "blk"), "chan"),
        P(),
        P(None, "chan"),
        P(None, "chan"),
        P(("mset", "blk"), "chan", None),
        P("chan", ("mset", "blk"), None),
        P(),
        P(),
    )
    return jax.shard_map(
        on_device,
        mesh=mesh,
        in_specs=placed,
        out_specs=P(None, None, ("mset", "blk"), "chan"),
        check_vma=False,
    )
```

profile of v0, /device:TPU:8, one launch (start us, length us, event | category | flops | bytes accessed | tf_op | source)
XLA Modules:
  0.0 190.6 jit_solution(135521996411559418)
XLA Ops:
  0.0 0.0 copy-start.4
  0.0 0.0 copy-start.3
  0.0 0.7 fusion.28
  0.7 0.7 convert_bitcast_fusion
  1.4 0.8 copy.33
  2.2 0.1 multiply_reduce_fusion
  2.3 0.8 compare_select_fusion
  3.2 3.7 %fusion.1 = bf16[24,1,8192]{2,0,1:T(8,128)(2,1)S(1)} fusion(bf16[24,384]{1,0:T(8,128)(2,1)S(1)} %convert_element_type.71, bf16[1,384,8192]{2,1,0:T(8,128)(2,1)} %param.12), kind=kOutput, calls=%fused_computation.2 | convolution fusion | flops 151191552 | bytes 6703104 | tf_op jit(solution)/shard_map/ijn,jnw->ijw/dot_general | solution.py:59
  6.9 13.8 %fusion = bf16[8,8192]{1,0:T(8,128)(2,1)S(1)} fusion(bf16[24,1,8192]{2,0,1:T(8,128)(2,1)S(1)} %fusion.1), kind=kCustom, calls=%all-reduce-scatter | all-reduce-scatter fusion | flops 262145 | bytes 525312
  20.8 3.6 %collective-permute-start = (bf16[6,8192]{1,0:T(8,128)(2,1)S(1)}, bf16[6,8192]{1,0:T(8,128)(2,1)S(1)}, u32[]{:S(2)}, u32[]{:S(2)}) collective-permute-start(bf16[6,8192]{1,0:T(8,128)(2,1)S(1)} %slice), channel_id=1, source_target_pairs={{0,64},{64,128},{128,192},{1,65},{65,129},{129,193},{2,66},{66,130... | collective-permute-start | bytes 294920
  24.4 0.0 copy-done.4
  24.4 0.1 broadcast_compare_fusion
  24.5 0.1 iota_compare_fusion
  24.6 0.0 copy-done.3
  24.6 0.1 broadcast_multiply_fusion.2
  24.7 0.1 broadcast_multiply_fusion.1
  24.8 1.4 fusion.16
  26.2 1.4 fusion.20
  27.6 7.1 %multiply_subtract_fusion = (f32[3,64,64,128]{3,2,1,0:T(8,128)}, f32[3,64,64,128]{3,2,1,0:T(8,128)}) fusion(f32[3,64,128]{2,1,0:T(8,128)S(1)} %get-tuple-element.12, f32[3,64,64]{2,1,0:T(8,128)S(1)} %get-tuple-element.10, f32[3,64,128]{2,1,0:T(8,128)S(1)} %get-tuple-element.11, f32[3,64,64]{2,1,0:T(8,128)S(1)} %get-tuple-element.9), kind=kLoop, calls=%fused_computation.10 | loop fusion | flops 9437184 | bytes 12877824 | tf_op jit(solution)/shard_map/vmap()/sub | solution.py:23
  34.7 7.2 %add.77 = f32[3,64,8192]{2,1,0:T(8,128)} reshape(f32[3,64,64,128]{3,2,1,0:T(8,128)} %get-tuple-element.8) | data formatting | bytes 12582912 | tf_op jit(solution)/shard_map/vmap()/add | solution.py:24
  41.8 0.0 copy-start.5
  41.8 7.2 %sub.15 = f32[3,64,8192]{2,1,0:T(8,128)} reshape(f32[3,64,64,128]{3,2,1,0:T(8,128)} %get-tuple-element.7) | data formatting | bytes 12582912 | tf_op jit(solution)/shard_map/vmap()/sub | solution.py:23
  49.0 0.0 copy-done.5
  49.0 0.6 dynamic-slice.4
  50.3 0.0 collective-permute-done
  50.3 0.4 concatenate.5
  50.7 0.1 dynamic-slice_bitcast_fusion
  50.7 6.9 %copy.35 = bf16[6,1,8192]{0,1,2:T(2,128)(2,1)} copy(bf16[6,1,8192]{2,0,1:T(8,128)(2,1)S(1)} %dynamic-slice_bitcast_fusion) | data formatting | bytes 196608 | tf_op jit(solution)/shard_map/reduce_scatter | solution.py:62
  57.6 0.5 broadcast.259
  58.1 45.2 %reduce.1 = bf16[8192,6]{1,0:T(8,128)(2,1)S(1)} reduce(bf16[8192,1,6]{2,1,0:T(2,128)(2,1)} %bitcast.55, bf16[]{:T(256)} %broadcast.259), dimensions={1}, to_apply=%bitcast.51.reduce_sub_computation | reduce | bytes 196610
  103.4 4.1 %reshape.214 = bf16[64,2,384]{2,1,0:T(2,128)(2,1)} reshape(bf16[8192,6]{1,0:T(8,128)(2,1)S(1)} %reduce.1) | data formatting | bytes 196608
  107.5 12.1 %all-to-all-start = ((bf16[64,2,384]{2,1,0:T(2,128)(2,1)}), bf16[64,2,384]{2,1,0:T(2,128)(2,1)S(1)}, u32[]{:S(2)}, u32[]{:S(2)}) async-start(bf16[64,2,384]{2,1,0:T(2,128)(2,1)} %reshape.214), calls=%async_computation | async-start | bytes 196608 | tf_op jit(solution)/shard_map/all_to_all | solution.py:65
  119.6 8.0 %select_convert_fusion.1 = (bf16[3,64,8192]{2,1,0:T(8,128)(2,1)S(1)}, bf16[3,64,8192]{2,1,0:T(8,128)(2,1)}) fusion(f32[3,64,8192]{2,1,0:T(8,128)} %sub.15, f32[64]{0:T(128)S(1)} %get-tuple-element.15, pred[3,8192]{1,0:T(4,128)(4,1)S(1)} %iota_compare_fusion, f32[3,64,8192]{2,1,0:T(8,128)} %add.77, f32[64]{0:T(128)S(1)} %get-tuple-element.16), kind=kLoop, calls=%fused_computation.9 | loop fusion | flops 9437184 | bytes 18899456 | tf_op jit(solution)/shard_map/convert
  127.6 1.6 all-to-all-done
  129.2 8.3 %reshape.215 = bf16[8192,1,6]{2,1,0:T(2,128)(2,1)} reshape(bf16[64,2,384]{2,1,0:T(2,128)(2,1)S(1)} %all-to-all-done) | data formatting | bytes 196608
  137.5 8.1 %copy.36 = bf16[6,1,8192]{2,0,1:T(8,128)(2,1)S(1)} copy(bf16[6,1,8192]{0,1,2:T(2,128)(2,1)} %bitcast.56) | data formatting | bytes 196608 | tf_op jit(solution)/shard_map/all_to_all | solution.py:65
  145.6 0.2 reshape.206
  145.8 6.8 %fusion.6 = bf16[3,128,128]{2,1,0:T(8,128)(2,1)S(1)} fusion(bf16[3,128,8192]{2,1,0:T(8,128)(2,1)} %param.13, bf16[3,128,128]{2,1,0:T(8,128)(2,1)S(1)} %reshape.206, bf16[3,64,8192]{2,1,0:T(8,128)(2,1)} %get-tuple-element.14, bf16[3,64,8192]{2,1,0:T(8,128)(2,1)S(1)} %get-tuple-element.13), kind=kOutput, calls=%fused_computation.12 | convolution fusion | flops 1645264896 | bytes 12779520 | tf_op jit(solution)/shard_map/cnp,crp->cnr/dot_general | solution.py:73
  152.6 0.0 copy-start
  152.6 0.0 copy-start.1
  152.6 0.0 copy-start.2
  152.7 0.1 copy.38
  152.7 18.6 %all_to_all.21 = bf16[6,64,128]{2,0,1:T(8,128)(2,1)S(1)} all-to-all(bf16[6,64,128]{2,0,1:T(8,128)(2,1)S(1)} %copy.38), channel_id=1, replica_groups=mesh['chan'=4,'mset'=8,'blk'=8] {'mset','blk'}, dimensions={1} | all-to-all | bytes 196608 | tf_op jit(solution)/shard_map/all_to_all | solution.py:75
  171.3 0.2 copy.39
  171.5 13.6 %all_gather.3 = bf16[24,1,8192]{2,1,0:T(2,128)(2,1)S(1)} all-gather(bf16[6,1,8192]{2,1,0:T(2,128)(2,1)S(1)} %copy.39), channel_id=1, replica_groups=mesh['chan'=4,'mset'=8,'blk'=8] {'chan'}, dimensions={0}, use_global_device_ids=true | all-gather | bytes 491520 | tf_op jit(solution)/shard_map/all_gather | solution.py:78
  185.1 4.6 %fusion.7 = f32[24,1,384]{2,0,1:T(8,128)S(1)} fusion(bf16[1,384,8192]{2,1,0:T(8,128)(2,1)} %param.12, bf16[24,1,8192]{2,1,0:T(2,128)(2,1)S(1)} %all_gather.3), kind=kOutput, calls=%fused_computation.13 | convolution fusion | flops 150994944 | bytes 6721536 | tf_op jit(solution)/shard_map/ogb,gfb->ogf/dot_general | solution.py:79
  189.8 0.0 copy-done
  189.8 0.0 copy-done.1
  189.8 0.0 copy-done.2
  189.8 0.2 fusion.10
  190.0 0.6 copy.41
  (12 shorter events, 0.2 us)
Async XLA Ops:
  0.0 24.4 %copy-start.4 = (s32[12]{0:T(128)S(1)}, s32[12]{0:T(128)}, u32[]{:S(2)}) copy-start(s32[12]{0:T(128)} %param.15) | copy-start | bytes 148
  0.0 24.6 %copy-start.3 = (s32[64]{0:T(128)S(1)}, s32[64]{0:T(128)}, u32[]{:S(2)}) copy-start(s32[64]{0:T(128)} %param.14) | copy-start | bytes 772
  20.8 29.5 %collective-permute-start = (bf16[6,8192]{1,0:T(8,128)(2,1)S(1)}, bf16[6,8192]{1,0:T(8,128)(2,1)S(1)}, u32[]{:S(2)}, u32[]{:S(2)}) collective-permute-start(bf16[6,8192]{1,0:T(8,128)(2,1)S(1)} %slice), channel_id=1, source_target_pairs={{0,64},{64,128},{128,192},{1,65},{65,129},{129,193},{2,66},{66,130... | collective-permute-start | bytes 294920
  41.8 7.2 %copy-start.5 = (u32[256]{0:T(256)S(1)}, u32[256]{0:T(256)}, u32[]{:S(2)}) copy-start(u32[256]{0:T(256)} %constant.68) | copy-start | bytes 3076
  107.5 21.7 %all-to-all-start = ((bf16[64,2,384]{2,1,0:T(2,128)(2,1)}), bf16[64,2,384]{2,1,0:T(2,128)(2,1)S(1)}, u32[]{:S(2)}, u32[]{:S(2)}) async-start(bf16[64,2,384]{2,1,0:T(2,128)(2,1)} %reshape.214), calls=%async_computation | async-start | bytes 196608 | tf_op jit(solution)/shard_map/all_to_all | solution.py:65
  152.6 37.2 %copy-start = (bf16[2,3,1,384]{3,0,2,1:T(2,128)(2,1)S(1)}, bf16[2,3,1,384]{3,0,2,1:T(2,128)(2,1)}, u32[]{:S(2)}) copy-start(bf16[2,3,1,384]{3,0,2,1:T(2,128)(2,1)} %param.8) | copy-start | bytes 13828
  152.6 37.2 %copy-start.1 = (f32[12,3]{0,1:T(4,128)S(1)}, f32[12,3]{0,1:T(4,128)}, u32[]{:S(2)}) copy-start(f32[12,3]{0,1:T(4,128)} %param.9) | copy-start | bytes 436
  152.6 37.2 %copy-start.2 = (f32[3,384]{1,0:T(4,128)S(1)}, f32[3,384]{1,0:T(4,128)}, u32[]{:S(2)}) copy-start(f32[3,384]{1,0:T(4,128)} %param.11) | copy-start | bytes 13828
where the time goes:
time: 192 us; the launch traced here: 191 us
  other arithmetic  65.8 us (34%)
  blocking collectives  46 us (24%)
  local copies, waits for them, and re-layouts  45.2 us (24%)
  starting transfers between devices  15.7 us (8%)
  matrix products  15.3 us (8%)
    unnamed x1, other arithmetic  45.2 us
    all_to_all x1, blocking collectives, on_device(): lax.all_to_all(mode_spectra, ('mset', 'blk'), split_axis=1, concat_axis=2...  18.6 us
    unnamed x20, local copies, waits for them, and re-layouts  14.8 us
    unnamed x1, blocking collectives  13.8 us
    all_gather x1, blocking collectives, on_device(): collected_rows = lax.all_gather(returned, 'chan', axis=0, tiled=True)  13.6 us
    all_to_all x1, starting transfers between devices, on_device(): lax.all_to_all(reduced_sum, ('mset', 'blk'), split_axis=2, concat_axis=1,...  12.1 us
    all_to_all x1, local copies, waits for them, and re-layouts, on_device(): lax.all_to_all(reduced_sum, ('mset', 'blk'), split_axis=2, concat_axis=1,...  8.11 us
    another operation x1, other arithmetic  7.99 us
  transfers between devices with their start and end apart: 2, of which 1 were waited for; matrix products, arithmetic and copies ran while one was open for 17% of the time, Pallas kernels for 0%

commit v1 on v0

--- a/solution.py
+++ b/solution.py
@@ -75,7 +75,12 @@
     returned = lax.all_to_all(
         mode_spectra, ("mset", "blk"), split_axis=1, concat_axis=2, tiled=True
     )
-    collected_rows = lax.all_gather(returned, "chan", axis=0, tiled=True)
+    ring = [returned]
+    for hop in range(3):
+        ring.append(lax.ppermute(ring[-1], "chan", [(dev, (dev + 1) % 4) for dev in range(4)]))
+    collected_rows = jnp.roll(
+        jnp.concatenate(ring[::-1], axis=0), (lax.axis_index("chan") + 1) * ring[0].shape[0], axis=0
+    )
     harmonic_back = jnp.einsum(
         "ogb,gfb->ogf", collected_rows, legendre, preferred_element_type=jnp.float32
     )

time: 192 us -> 198 us (1.031)
  waiting for transfers between devices: 1.63 us -> 20.1 us
  blocking collectives: 46 us -> 32.4 us
    ppermute x0 -> x3, waiting for transfers between devices: none -> 18.5 us  [on_device(): lax.ppermute(ring[-1], 'chan', [(dev, (dev + 1) % 4) for dev in range(4)])]
    all_gather x1 -> x0, blocking collectives: 13.6 us -> none  [on_device(): collected_rows = lax.all_gather(returned, 'chan', axis=0, tiled=True)]
  transfers between devices with their start and end apart: 2 -> 5, of which waited for: 1 -> 4; matrix products, arithmetic and copies ran while one was open for 17% -> 17% of each run, Pallas kernels for 0% -> 0%
where the time goes in v1:
time: 198 us; the launch traced here: 197 us
  other arithmetic  65.8 us (33%)
  local copies, waits for them, and re-layouts  46.7 us (24%)
  blocking collectives  32.4 us (16%)
  waiting for transfers between devices  20.1 us (10%)
  starting transfers between devices  15.7 us (8%)
  matrix products  15.2 us (8%)
    unnamed x1, other arithmetic  45.2 us
    all_to_all x1, blocking collectives, on_device(): lax.all_to_all(mode_spectra, ('mset', 'blk'), split_axis=1, concat_axis=2...  18.6 us
    ppermute x3, waiting for transfers between devices, on_device(): lax.ppermute(ring[-1], 'chan', [(dev, (dev + 1) % 4) for dev in range(4)])  18.5 us
    unnamed x20, local copies, waits for them, and re-layouts  14.8 us
    unnamed x1, blocking collectives  13.8 us
    all_to_all x1, starting transfers between devices, on_device(): lax.all_to_all(reduced_sum, ('mset', 'blk'), split_axis=2, concat_axis=1,...  12.1 us
    all_to_all x1, local copies, waits for them, and re-layouts, on_device(): lax.all_to_all(reduced_sum, ('mset', 'blk'), split_axis=2, concat_axis=1,...  8.11 us
    another operation x1, other arithmetic  7.97 us
  transfers between devices with their start and end apart: 5, of which 4 were waited for; matrix products, arithmetic and copies ran while one was open for 17% of the time, Pallas kernels for 0%

profile of v1, /device:TPU:8, one launch (start us, length us, event | category | flops | bytes accessed | tf_op | source)
XLA Modules:
  0.0 196.9 jit_solution(14186186511561413064)
XLA Ops:
  0.0 0.0 copy-start.4
  0.0 0.0 copy-start.3
  0.0 0.7 fusion.28
  0.7 0.7 convert_bitcast_fusion
  1.4 0.8 copy.32
  2.2 0.1 multiply_reduce_fusion
  2.3 0.8 compare_select_fusion
  3.2 3.7 %fusion.1 = bf16[24,1,8192]{2,0,1:T(8,128)(2,1)S(1)} fusion(bf16[24,384]{1,0:T(8,128)(2,1)S(1)} %convert_element_type.71, bf16[1,384,8192]{2,1,0:T(8,128)(2,1)} %param.12), kind=kOutput, calls=%fused_computation.2 | convolution fusion | flops 151191552 | bytes 6703104 | tf_op jit(solution)/shard_map/ijn,jnw->ijw/dot_general | solution.py:59
  6.9 13.8 %fusion = bf16[8,8192]{1,0:T(8,128)(2,1)S(1)} fusion(bf16[24,1,8192]{2,0,1:T(8,128)(2,1)S(1)} %fusion.1), kind=kCustom, calls=%all-reduce-scatter | all-reduce-scatter fusion | flops 262145 | bytes 525312
  20.8 3.6 %collective-permute-start.3 = (bf16[6,8192]{1,0:T(8,128)(2,1)S(1)}, bf16[6,8192]{1,0:T(8,128)(2,1)S(1)}, u32[]{:S(2)}, u32[]{:S(2)}) collective-permute-start(bf16[6,8192]{1,0:T(8,128)(2,1)S(1)} %slice), channel_id=1, source_target_pairs={{0,64},{64,128},{128,192},{1,65},{65,129},{129,193},{2,66},{66,130... | collective-permute-start | bytes 294920
  24.4 0.0 copy-done.4
  24.4 0.1 broadcast_compare_fusion
  24.5 0.1 iota_compare_fusion
  24.6 0.0 copy-done.3
  24.6 0.1 broadcast_multiply_fusion.2
  24.7 0.1 broadcast_multiply_fusion.1
  24.8 1.4 fusion.16
  26.2 1.4 fusion.20
  27.6 7.1 %multiply_subtract_fusion = (f32[3,64,64,128]{3,2,1,0:T(8,128)}, f32[3,64,64,128]{3,2,1,0:T(8,128)}) fusion(f32[3,64,128]{2,1,0:T(8,128)S(1)} %get-tuple-element.12, f32[3,64,64]{2,1,0:T(8,128)S(1)} %get-tuple-element.10, f32[3,64,128]{2,1,0:T(8,128)S(1)} %get-tuple-element.11, f32[3,64,64]{2,1,0:T(8,128)S(1)} %get-tuple-element.9), kind=kLoop, calls=%fused_computation.10 | loop fusion | flops 9437184 | bytes 12877824 | tf_op jit(solution)/shard_map/vmap()/sub | solution.py:23
  34.6 7.2 %add.90 = f32[3,64,8192]{2,1,0:T(8,128)} reshape(f32[3,64,64,128]{3,2,1,0:T(8,128)} %get-tuple-element.8) | data formatting | bytes 12582912 | tf_op jit(solution)/shard_map/vmap()/add | solution.py:24
  41.8 0.0 copy-start.5
  41.8 7.2 %sub.19 = f32[3,64,8192]{2,1,0:T(8,128)} reshape(f32[3,64,64,128]{3,2,1,0:T(8,128)} %get-tuple-element.7) | data formatting | bytes 12582912 | tf_op jit(solution)/shard_map/vmap()/sub | solution.py:23
  49.0 0.0 copy-done.5
  49.0 0.6 dynamic-slice.4
  50.2 0.0 collective-permute-done.3
  50.3 0.4 concatenate.12
  50.6 0.1 dynamic-slice_bitcast_fusion
  50.7 6.9 %copy.34 = bf16[6,1,8192]{0,1,2:T(2,128)(2,1)} copy(bf16[6,1,8192]{2,0,1:T(8,128)(2,1)S(1)} %dynamic-slice_bitcast_fusion) | data formatting | bytes 196608 | tf_op jit(solution)/shard_map/reduce_scatter | solution.py:62
  57.6 0.5 broadcast.259
  58.1 45.2 %reduce.1 = bf16[8192,6]{1,0:T(8,128)(2,1)S(1)} reduce(bf16[8192,1,6]{2,1,0:T(2,128)(2,1)} %bitcast.55, bf16[]{:T(256)} %broadcast.259), dimensions={1}, to_apply=%bitcast.51.reduce_sub_computation | reduce | bytes 196610
  103.3 4.1 %reshape.214 = bf16[64,2,384]{2,1,0:T(2,128)(2,1)} reshape(bf16[8192,6]{1,0:T(8,128)(2,1)S(1)} %reduce.1) | data formatting | bytes 196608
  107.5 12.1 %all-to-all-start = ((bf16[64,2,384]{2,1,0:T(2,128)(2,1)}), bf16[64,2,384]{2,1,0:T(2,128)(2,1)S(1)}, u32[]{:S(2)}, u32[]{:S(2)}) async-start(bf16[64,2,384]{2,1,0:T(2,128)(2,1)} %reshape.214), calls=%async_computation | async-start | bytes 196608 | tf_op jit(solution)/shard_map/all_to_all | solution.py:65
  119.6 8.0 %select_convert_fusion.1 = (bf16[3,64,8192]{2,1,0:T(8,128)(2,1)S(1)}, bf16[3,64,8192]{2,1,0:T(8,128)(2,1)}) fusion(f32[3,64,8192]{2,1,0:T(8,128)} %sub.19, f32[64]{0:T(128)S(1)} %get-tuple-element.15, pred[3,8192]{1,0:T(4,128)(4,1)S(1)} %iota_compare_fusion, f32[3,64,8192]{2,1,0:T(8,128)} %add.90, f32[64]{0:T(128)S(1)} %get-tuple-element.16), kind=kLoop, calls=%fused_computation.9 | loop fusion | flops 9437184 | bytes 18899456 | tf_op jit(solution)/shard_map/convert
  127.6 1.6 all-to-all-done
  129.2 8.3 %reshape.215 = bf16[8192,1,6]{2,1,0:T(2,128)(2,1)} reshape(bf16[64,2,384]{2,1,0:T(2,128)(2,1)S(1)} %all-to-all-done) | data formatting | bytes 196608
  137.4 8.1 %copy.35 = bf16[6,1,8192]{2,0,1:T(8,128)(2,1)S(1)} copy(bf16[6,1,8192]{0,1,2:T(2,128)(2,1)} %bitcast.56) | data formatting | bytes 196608 | tf_op jit(solution)/shard_map/all_to_all | solution.py:65
  145.5 0.2 reshape.206
  145.7 6.8 %fusion.6 = bf16[3,128,128]{2,1,0:T(8,128)(2,1)S(1)} fusion(bf16[3,128,8192]{2,1,0:T(8,128)(2,1)} %param.13, bf16[3,128,128]{2,1,0:T(8,128)(2,1)S(1)} %reshape.206, bf16[3,64,8192]{2,1,0:T(8,128)(2,1)} %get-tuple-element.14, bf16[3,64,8192]{2,1,0:T(8,128)(2,1)S(1)} %get-tuple-element.13), kind=kOutput, calls=%fused_computation.12 | convolution fusion | flops 1645264896 | bytes 12779520 | tf_op jit(solution)/shard_map/cnp,crp->cnr/dot_general | solution.py:73
  152.5 0.0 copy-start
  152.5 0.0 copy-start.1
  152.5 0.0 copy-start.2
  152.5 0.1 copy.37
  152.6 18.6 %all_to_all.21 = bf16[6,64,128]{2,0,1:T(8,128)(2,1)S(1)} all-to-all(bf16[6,64,128]{2,0,1:T(8,128)(2,1)S(1)} %copy.37), channel_id=1, replica_groups=mesh['chan'=4,'mset'=8,'blk'=8] {'mset','blk'}, dimensions={1} | all-to-all | bytes 196608 | tf_op jit(solution)/shard_map/all_to_all | solution.py:75
  171.2 0.0 collective-permute-start
  171.2 6.2 %collective-permute-done = bf16[6,1,8192]{2,0,1:T(8,128)(2,1)S(1)} collective-permute-done((bf16[6,1,8192]{2,0,1:T(8,128)(2,1)S(1)}, bf16[6,1,8192]{2,0,1:T(8,128)(2,1)S(1)}, u32[]{:S(2)}, u32[]{:S(2)}) %collective-permute-start) | collective-permute-done | bytes 98336 | tf_op jit(solution)/shard_map/ppermute | solution.py:80
  177.4 0.0 collective-permute-start.1
  177.4 6.2 %collective-permute-done.1 = bf16[6,1,8192]{2,0,1:T(8,128)(2,1)S(1)} collective-permute-done((bf16[6,1,8192]{2,0,1:T(8,128)(2,1)S(1)}, bf16[6,1,8192]{2,0,1:T(8,128)(2,1)S(1)}, u32[]{:S(2)}, u32[]{:S(2)}) %collective-permute-start.1) | collective-permute-done | bytes 98336 | tf_op jit(solution)/shard_map/ppermute | solution.py:80
  183.6 0.0 collective-permute-start.2
  183.6 6.2 %collective-permute-done.2 = bf16[6,1,8192]{2,0,1:T(8,128)(2,1)S(1)} collective-permute-done((bf16[6,1,8192]{2,0,1:T(8,128)(2,1)S(1)}, bf16[6,1,8192]{2,0,1:T(8,128)(2,1)S(1)}, u32[]{:S(2)}, u32[]{:S(2)}) %collective-permute-start.2) | collective-permute-done | bytes 98336 | tf_op jit(solution)/shard_map/ppermute | solution.py:80
  189.8 1.6 concatenate.11
  191.4 4.5 %fusion.7 = f32[24,1,384]{2,0,1:T(8,128)S(1)} fusion(bf16[1,384,8192]{2,1,0:T(8,128)(2,1)} %param.12, bf16[48,1,8192]{2,0,1:T(8,128)(2,1)S(1)} %concatenate.11, s32[]{:T(128)S(6)} %select_n.75), kind=kOutput, calls=%fused_computation.13 | convolution fusion | flops 150994944 | bytes 6721540 | tf_op jit(solution)/shard_map/ogb,gfb->ogf/dot_general | solution.py:84
  196.1 0.0 copy-done
  196.1 0.0 copy-done.1
  196.1 0.0 copy-done.2
  196.1 0.2 fusion.10
  196.3 0.6 copy.39
  (12 shorter events, 0.2 us)
Async XLA Ops:
  0.0 24.4 %copy-start.4 = (s32[12]{0:T(128)S(1)}, s32[12]{0:T(128)}, u32[]{:S(2)}) copy-start(s32[12]{0:T(128)} %param.15) | copy-start | bytes 148
  0.0 24.6 %copy-start.3 = (s32[64]{0:T(128)S(1)}, s32[64]{0:T(128)}, u32[]{:S(2)}) copy-start(s32[64]{0:T(128)} %param.14) | copy-start | bytes 772
  20.8 29.5 %collective-permute-start.3 = (bf16[6,8192]{1,0:T(8,128)(2,1)S(1)}, bf16[6,8192]{1,0:T(8,128)(2,1)S(1)}, u32[]{:S(2)}, u32[]{:S(2)}) collective-permute-start(bf16[6,8192]{1,0:T(8,128)(2,1)S(1)} %slice), channel_id=1, source_target_pairs={{0,64},{64,128},{128,192},{1,65},{65,129},{129,193},{2,66},{66,130... | collective-permute-start | bytes 294920
  41.8 7.2 %copy-start.5 = (u32[256]{0:T(256)S(1)}, u32[256]{0:T(256)}, u32[]{:S(2)}) copy-start(u32[256]{0:T(256)} %constant.89) | copy-start | bytes 3076
  107.5 21.7 %all-to-all-start = ((bf16[64,2,384]{2,1,0:T(2,128)(2,1)}), bf16[64,2,384]{2,1,0:T(2,128)(2,1)S(1)}, u32[]{:S(2)}, u32[]{:S(2)}) async-start(bf16[64,2,384]{2,1,0:T(2,128)(2,1)} %reshape.214), calls=%async_computation | async-start | bytes 196608 | tf_op jit(solution)/shard_map/all_to_all | solution.py:65
  152.5 43.6 %copy-start = (bf16[2,3,1,384]{3,0,2,1:T(2,128)(2,1)S(1)}, bf16[2,3,1,384]{3,0,2,1:T(2,128)(2,1)}, u32[]{:S(2)}) copy-start(bf16[2,3,1,384]{3,0,2,1:T(2,128)(2,1)} %param.8) | copy-start | bytes 13828
  152.5 43.5 %copy-start.1 = (f32[12,3]{0,1:T(4,128)S(1)}, f32[12,3]{0,1:T(4,128)}, u32[]{:S(2)}) copy-start(f32[12,3]{0,1:T(4,128)} %param.9) | copy-start | bytes 436
  152.5 43.5 %copy-start.2 = (f32[3,384]{1,0:T(4,128)S(1)}, f32[3,384]{1,0:T(4,128)}, u32[]{:S(2)}) copy-start(f32[3,384]{1,0:T(4,128)} %param.11) | copy-start | bytes 13828
  171.2 6.2 %collective-permute-start = (bf16[6,1,8192]{2,0,1:T(8,128)(2,1)S(1)}, bf16[6,1,8192]{2,0,1:T(8,128)(2,1)S(1)}, u32[]{:S(2)}, u32[]{:S(2)}) collective-permute-start(bf16[6,1,8192]{2,0,1:T(8,128)(2,1)S(1)} %bitcast.57), channel_id=1, source_target_pairs={{0,64},{64,128},{128,192},{192,0},{1,65},{65,129},{129,193},{193,1... | collective-permute-start | bytes 294920 | tf_op jit(solution)/shard_map/ppermute | solution.py:80
  177.4 6.2 %collective-permute-start.1 = (bf16[6,1,8192]{2,0,1:T(8,128)(2,1)S(1)}, bf16[6,1,8192]{2,0,1:T(8,128)(2,1)S(1)}, u32[]{:S(2)}, u32[]{:S(2)}) collective-permute-start(bf16[6,1,8192]{2,0,1:T(8,128)(2,1)S(1)} %collective-permute-done), channel_id=1, source_target_pairs={{0,64},{64,128},{128,192},{192,0},{1,65},{65,129},{129,193},{193,1... | collective-permute-start | bytes 294920 | tf_op jit(solution)/shard_map/ppermute | solution.py:80
  183.6 6.2 %collective-permute-start.2 = (bf16[6,1,8192]{2,0,1:T(8,128)(2,1)S(1)}, bf16[6,1,8192]{2,0,1:T(8,128)(2,1)S(1)}, u32[]{:S(2)}, u32[]{:S(2)}) collective-permute-start(bf16[6,1,8192]{2,0,1:T(8,128)(2,1)S(1)} %collective-permute-done.1), channel_id=1, source_target_pairs={{0,64},{64,128},{128,192},{192,0},{1,65},{65,129},{129,193},{193,1... | collective-permute-start | bytes 294920 | tf_op jit(solution)/shard_map/ppermute | solution.py:80
